TPU v7x, 32 devices: a whole 2x2x4 slice. The times are simulated.
32 devices in a mesh: rep: 2 (over core), shard: 16 (over z, y, x).
Axes of the slice: x: 2, y: 2, z: 4, core: 2. Of those that a mesh axis runs over, the one named last changes fastest.
Arguments:
- tokens: bfloat16 [32, 1024, 768], P('rep', 'shard'), may hold values from -6 to 6
- cotangent: bfloat16 [32, 1024, 768], P('rep', 'shard'), may hold values from -6 to 6
- lengths: int32 [2, 16], P('rep'), may hold values from 512 to 1024, as said below
- order: int32 [2, 16], P('rep'), may hold values from 0 to 15, each once within a row
- norm_weight: bfloat16 [768], P('shard'), may hold values from 0.099609375 to 1.8984375
- in_weight: bfloat16 [768, 3352], P('shard'), may hold values from -0.21875 to 0.21875
- conv_weight: bfloat16 [1792, 4], P('shard'), may hold values from -3 to 3
- conv_bias: bfloat16 [1792], P('shard'), may hold values from -3 to 3
- step_bias: float32 [24], replicated, may hold values from -5.5 to -2.5
- decay_log: float32 [24], replicated, may hold values from 0 to 2.77
- skip_gain: float32 [24], replicated, may hold values from 0.5 to 1.5
- gate_norm_weight: bfloat16 [1536], P('shard'), may hold values from 0.099609375 to 1.8984375
- out_weight: bfloat16 [1536, 768], P('shard'), may hold values from -0.15625 to 0.15625
Outputs:
- output: bfloat16 [32, 1024, 768], P('rep', 'shard')
- input_grad: bfloat16 [32, 1024, 768], P('rep', 'shard')
- grad_norm: float32 [768], P('shard')
- grad_in: float32 [768, 3352], P('shard')
- grad_conv: float32 [1792, 4], P('shard')
- grad_conv_bias: float32 [1792], P('shard')
- grad_step_bias: float32 [24], replicated
- grad_decay_log: float32 [24], replicated
- grad_skip: float32 [24], replicated
- grad_gate_norm: float32 [1536], P('shard')
- grad_out: float32 [1536, 768], P('shard')
Inputs may be any that keep to these rules, and one draw needn't show every extreme that they name: Each row of order holds every number from 0 to 15 once: slot k of group r holds sequence order[r, k]. lengths[r, s] counts the valid leading positions of sequence s of group r; each row has one entry equal to 1024 and one equal to 512.
All inputs are finite; a program needn't handle non-finite values.
Results may differ from a plain program's by a relative error of at most 0.012.
The roundings to bfloat16 on the way count: a program that leaves them out, or rounds other values in their place, can miss the bound.
Values may be sent and summed in bfloat16 or wider, within the bound.
A program may use at most 192 MiB of HBM per device.

v0:
```python
import jax
import jax.numpy as jnp
from jax import lax
from jax.sharding import PartitionSpec as P

HEADS = 24
HEADDIM = 64
STATE = 128
CONV = 4
SPAN = 256
DI = 1536
XBC = 1792
epsilon = 1e-05


def decay_terms(log_block, step_block):
    cumul = jnp.cumsum(log_block, axis=0)
    cumul_heads = cumul.T
    positions = log_block.shape[0]
    causal = jnp.arange(positions)[:, None] >= jnp.arange(positions)[None, :]
    spread = jnp.where(causal[None], cumul_heads[:, :, None] - cumul_heads[:, None, :], 0.0)
    factor = jnp.where(causal[None], jnp.exp(spread), 0.0) * step_block.T[:, None, :]
    carry_weight = jnp.exp(cumul[-1][None, :] - cumul) * step_block
    return (factor, carry_weight, jnp.exp(cumul), jnp.exp(cumul[-1]))


def norm_part(tok_float, norm_gain):
    return (
        tok_float
        * lax.rsqrt(jnp.mean(tok_float * tok_float, axis=-1, keepdims=True) + epsilon)
        * norm_gain
    )


def conv_part(conv_in, conv_taps, conv_shift):
    length = conv_in.shape[0]
    padded = jnp.concatenate(
        [jnp.zeros((CONV - 1, conv_in.shape[1]), jnp.float32), conv_in], axis=0
    )
    total = conv_shift[None, :] + jnp.zeros_like(conv_in)
    for tap in range(CONV):
        total = total + conv_taps[:, tap][None, :] * padded[tap : tap + length]
    return jax.nn.silu(total)


def step_part(step_raw, step_bias, decay_log):
    step_size = jax.nn.softplus(step_raw + step_bias[None, :])
    return (step_size, -jnp.exp(decay_log)[None, :] * step_size)


def gate_part(scan_out, heads_in, skip_gain, gate_raw, gate_gain):
    mixed = scan_out + jnp.repeat(skip_gain, HEADDIM)[None, :] * heads_in
    gated = mixed * jax.nn.silu(gate_raw)
    return gated * lax.rsqrt(jnp.mean(gated * gated, axis=-1, keepdims=True) + epsilon) * gate_gain


def block_forward(state, inputs):
    heads_blk, keys_blk, query_blk, step_blk, log_blk = inputs
    factor, carry_weight, growth, growth_last = decay_terms(log_blk, step_blk)
    scores = jnp.einsum("tn,sn->ts", query_blk, keys_blk, preferred_element_type=jnp.float32)
    mixing = (scores[None] * factor).astype(jnp.bfloat16)
    within = jnp.einsum("hts,shp->thp", mixing, heads_blk, preferred_element_type=jnp.float32)
    across = jnp.einsum(
        "tn,hpn->thp", query_blk, state.astype(jnp.bfloat16), preferred_element_type=jnp.float32
    )
    result = within + growth[:, :, None] * across
    weighted = (heads_blk.astype(jnp.float32) * carry_weight[:, :, None]).astype(jnp.bfloat16)
    contrib = jnp.einsum("sn,shp->hpn", keys_blk, weighted, preferred_element_type=jnp.float32)
    return (growth_last[:, None, None] * state + contrib, (result, state))


def block_backward(later, inputs):
    heads_blk, keys_blk, query_blk, step_blk, log_blk, grad_blk, state = inputs
    terms, decay_pull = jax.vjp(decay_terms, log_blk, step_blk)
    factor, carry_weight, growth, growth_last = terms
    scores = jnp.einsum("tn,sn->ts", query_blk, keys_blk, preferred_element_type=jnp.float32)
    mixing = (scores[None] * factor).astype(jnp.bfloat16)
    state_low = state.astype(jnp.bfloat16)
    across = jnp.einsum("tn,hpn->thp", query_blk, state_low, preferred_element_type=jnp.float32)
    heads_float = heads_blk.astype(jnp.float32)
    weighted = (heads_float * carry_weight[:, :, None]).astype(jnp.bfloat16)
    grad_within = grad_blk.astype(jnp.bfloat16)
    grad_across = (growth[:, :, None] * grad_blk).astype(jnp.bfloat16)
    grad_mixing = jnp.einsum(
        "thp,shp->hts", grad_within, heads_blk, preferred_element_type=jnp.float32
    )
    grad_heads = jnp.einsum("hts,thp->shp", mixing, grad_within, preferred_element_type=jnp.float32)
    grad_query = jnp.einsum(
        "thp,hpn->tn", grad_across, state_low, preferred_element_type=jnp.float32
    )
    grad_state = jnp.einsum(
        "thp,tn->hpn", grad_across, query_blk, preferred_element_type=jnp.float32
    )
    grad_state = grad_state + growth_last[:, None, None] * later
    grad_growth = jnp.sum(grad_blk * across, axis=2)
    later_low = later.astype(jnp.bfloat16)
    grad_weighted = jnp.einsum(
        "hpn,sn->shp", later_low, keys_blk, preferred_element_type=jnp.float32
    )
    grad_keys = jnp.einsum("hpn,shp->sn", later_low, weighted, preferred_element_type=jnp.float32)
    grad_heads = grad_heads + grad_weighted * carry_weight[:, :, None]
    grad_carry = jnp.sum(grad_weighted * heads_float, axis=2)
    grad_last = jnp.sum(later * state, axis=(1, 2))
    grad_scores = jnp.sum(grad_mixing * factor, axis=0).astype(jnp.bfloat16)
    grad_query = grad_query + jnp.dot(grad_scores, keys_blk, preferred_element_type=jnp.float32)
    grad_keys = grad_keys + jnp.einsum(
        "ts,tn->sn", grad_scores, query_blk, preferred_element_type=jnp.float32
    )
    grad_log, grad_step = decay_pull(
        (grad_mixing * scores[None], grad_carry, grad_growth, grad_last)
    )
    return (grad_state, (grad_heads, grad_keys, grad_query, grad_step, grad_log))


def forward_seq(
    tok_float,
    keep,
    norm_full,
    in_full,
    conv_full,
    shift_full,
    gate_full,
    out_full,
    step_bias,
    decay_log,
    skip_gain,
):
    seq_len = tok_float.shape[0]
    normed, norm_pull = jax.vjp(norm_part, tok_float, norm_full.astype(jnp.float32))
    normed_low = normed.astype(jnp.bfloat16)
    projected = jnp.dot(normed_low, in_full, preferred_element_type=jnp.float32)
    gate_raw = projected[:, :DI]
    conv_in = projected[:, DI : DI + XBC]
    step_raw = projected[:, DI + XBC :]
    convolved, conv_pull = jax.vjp(
        conv_part, conv_in, conv_full.astype(jnp.float32), shift_full.astype(jnp.float32)
    )
    heads_in = convolved[:, :DI]
    heads_low = heads_in.astype(jnp.bfloat16)
    key_low = convolved[:, DI : DI + STATE].astype(jnp.bfloat16)
    query_low = convolved[:, DI + STATE :].astype(jnp.bfloat16)
    decays, step_pull = jax.vjp(step_part, step_raw, step_bias, decay_log)
    step_size, log_decay = decays
    count = seq_len // SPAN
    blocks = (
        heads_low.reshape(count, SPAN, HEADS, HEADDIM),
        key_low.reshape(count, SPAN, STATE),
        query_low.reshape(count, SPAN, STATE),
        step_size.reshape(count, SPAN, HEADS),
        log_decay.reshape(count, SPAN, HEADS),
    )
    start = jnp.zeros((HEADS, HEADDIM, STATE), jnp.float32)
    final_state, kept = lax.scan(block_forward, start, blocks)
    scan_blocks, states = kept
    scan_out = scan_blocks.reshape(seq_len, DI)
    gate_value, gate_pull = jax.vjp(
        gate_part, scan_out, heads_in, skip_gain, gate_raw, gate_full.astype(jnp.float32)
    )
    gate_low = gate_value.astype(jnp.bfloat16)
    branch = jnp.dot(gate_low, out_full, preferred_element_type=jnp.float32)
    result = (tok_float + keep[:, None] * branch).astype(jnp.bfloat16)
    saved = (keep, normed_low, norm_pull, conv_pull, step_pull, gate_pull, gate_low, blocks, states)
    return (result, saved)


def backward_seq(saved, cot_float, in_full, out_full):
    keep, normed_low, norm_pull, conv_pull, step_pull, gate_pull, gate_low, blocks, states = saved
    seq_len = cot_float.shape[0]
    count = seq_len // SPAN
    grad_branch = (keep[:, None] * cot_float).astype(jnp.bfloat16)
    grad_out_full = jnp.einsum(
        "ti,tj->ij", gate_low, grad_branch, preferred_element_type=jnp.float32
    )
    grad_gate = jnp.einsum("tj,ij->ti", grad_branch, out_full, preferred_element_type=jnp.float32)
    grad_scan, grad_heads_skip, grad_skip, grad_gate_raw, grad_gate_gain = gate_pull(grad_gate)
    grad_scan_blocks = grad_scan.reshape(count, SPAN, HEADS, HEADDIM)
    first_grad, grads = lax.scan(
        block_backward,
        jnp.zeros((HEADS, HEADDIM, STATE), jnp.float32),
        (blocks[0], blocks[1], blocks[2], blocks[3], blocks[4], grad_scan_blocks, states),
        reverse=True,
    )
    grad_heads, grad_keys, grad_query, grad_step, grad_log = grads
    grad_step_raw, grad_step_bias, grad_decay_log = step_pull(
        (grad_step.reshape(seq_len, HEADS), grad_log.reshape(seq_len, HEADS))
    )
    grad_convolved = jnp.concatenate(
        [
            grad_heads.reshape(seq_len, DI) + grad_heads_skip,
            grad_keys.reshape(seq_len, STATE),
            grad_query.reshape(seq_len, STATE),
        ],
        axis=1,
    )
    grad_conv_in, grad_taps, grad_shift = conv_pull(grad_convolved)
    grad_projected = jnp.concatenate([grad_gate_raw, grad_conv_in, grad_step_raw], axis=1).astype(
        jnp.bfloat16
    )
    grad_in_full = jnp.einsum(
        "ti,tj->ij", normed_low, grad_projected, preferred_element_type=jnp.float32
    )
    grad_normed = jnp.einsum(
        "tj,ij->ti", grad_projected, in_full, preferred_element_type=jnp.float32
    )
    grad_tok, grad_norm_gain = norm_pull(grad_normed)
    input_grad = (cot_float + grad_tok).astype(jnp.bfloat16)
    weight_grads = (
        grad_norm_gain,
        grad_in_full,
        grad_taps,
        grad_shift,
        grad_gate_gain,
        grad_out_full,
    )
    return (input_grad, weight_grads, (grad_step_bias, grad_decay_log, grad_skip))


def on_device(
    tokens,
    cotangent,
    lengths,
    order,
    norm_weight,
    in_weight,
    conv_weight,
    conv_bias,
    step_bias,
    decay_log,
    skip_gain,
    gate_norm_weight,
    out_weight,
):
    peers = lax.axis_size("shard")
    rank = lax.axis_index("shard")
    slots = jnp.arange(peers, dtype=jnp.int32)
    order_row = order[0]
    inverse = jnp.sum(jnp.where(order_row[None, :] == slots[:, None], slots[None, :], 0), axis=1)
    piece = tokens.shape[1]
    width = tokens.shape[2]
    sent_tokens = jnp.take(tokens, inverse, axis=0).reshape(peers, 1, piece, width)
    sent_cot = jnp.take(cotangent, inverse, axis=0).reshape(peers, 1, piece, width)
    got_tokens, got_cot = (
        lax.all_to_all(sent_tokens, "shard", split_axis=0, concat_axis=2, tiled=True),
        lax.all_to_all(sent_cot, "shard", split_axis=0, concat_axis=2, tiled=True),
    )
    seq_len = got_tokens.shape[2]
    length_row = lengths[0]
    gathered = (
        lax.all_gather(norm_weight, "shard", axis=0, tiled=True),
        lax.all_gather(in_weight, "shard", axis=0, tiled=True),
        lax.all_gather(conv_weight, "shard", axis=0, tiled=True),
        lax.all_gather(conv_bias, "shard", axis=0, tiled=True),
        lax.all_gather(gate_norm_weight, "shard", axis=0, tiled=True),
        lax.all_gather(out_weight, "shard", axis=0, tiled=True),
    )
    norm_full, in_full, conv_full, shift_full, gate_full, out_full = gathered
    valid = length_row[rank]
    keep = (jnp.arange(seq_len, dtype=jnp.int32) < valid).astype(jnp.float32)
    forward_out, saved = forward_seq(
        got_tokens[0, 0].astype(jnp.float32),
        keep,
        norm_full,
        in_full,
        conv_full,
        shift_full,
        gate_full,
        out_full,
        step_bias,
        decay_log,
        skip_gain,
    )
    result = forward_out[None]
    grad_seq, weight_grads, head_terms = backward_seq(
        saved, got_cot[0, 0].astype(jnp.float32), in_full, out_full
    )
    input_grad = grad_seq[None]
    back_out, back_grad = (
        lax.all_to_all(result, "shard", split_axis=1, concat_axis=0, tiled=True),
        lax.all_to_all(input_grad, "shard", split_axis=1, concat_axis=0, tiled=True),
    )
    output = jnp.take(back_out, order_row, axis=0)
    input_back = jnp.take(back_grad, order_row, axis=0)
    summed = lax.psum(
        (
            weight_grads[0],
            weight_grads[1],
            weight_grads[2],
            weight_grads[3],
            weight_grads[4],
            weight_grads[5],
        ),
        "rep",
    )
    pieces = (
        lax.psum_scatter(summed[0], "shard", scatter_dimension=0, tiled=True),
        lax.psum_scatter(summed[1], "shard", scatter_dimension=0, tiled=True),
        lax.psum_scatter(summed[2], "shard", scatter_dimension=0, tiled=True),
        lax.psum_scatter(summed[3], "shard", scatter_dimension=0, tiled=True),
        lax.psum_scatter(summed[4], "shard", scatter_dimension=0, tiled=True),
        lax.psum_scatter(summed[5], "shard", scatter_dimension=0, tiled=True),
    )
    head_sums = lax.psum((head_terms[0], head_terms[1], head_terms[2]), ("rep", "shard"))
    return (
        output,
        input_back,
        pieces[0],
        pieces[1],
        pieces[2],
        pieces[3],
        head_sums[0],
        head_sums[1],
        head_sums[2],
        pieces[4],
        pieces[5],
    )


def solution(mesh):
    placed = (
        P("rep", "shard", None),
        P("rep", "shard", None),
        P("rep", None),
        P("rep", None),
        P("shard"),
        P("shard", None),
        P("shard", None),
        P("shard"),
        P(),
        P(),
        P(),
        P("shard"),
        P("shard", None),
    )
    return jax.shard_map(
        on_device,
        mesh=mesh,
        in_specs=placed,
        out_specs=(
            P("rep", "shard", None),
            P("rep", "shard", None),
            P("shard"),
            P("shard", None),
            P("shard", None),
            P("shard"),
            P(),
            P(),
            P(),
            P("shard"),
            P("shard", None),
        ),
        check_vma=False,
    )
```

profile of v0, /device:TPU:0, one launch (start us, length us, event | category | flops | bytes accessed | tf_op | source)
XLA Modules:
  0.0 1286.4 jit_solution(3603219273039151114)
XLA Ops:
  15.6 65.5 %all_to_all.42 = bf16[16,1,64,768]{3,2,1,0:T(8,128)(2,1)S(1)} all-to-all(bf16[16,1,64,768]{3,2,1,0:T(8,128)(2,1)S(1)} %get-tuple-element.698), channel_id=1, replica_groups=mesh['rep'=2,'shard'=16] {'shard'}, dimensions={0} | all-to-all | bytes 3145728 | tf_op jit(solution)/shard_map/all_to_all | solution.py:243
  89.8 115.9 %all-reduce.21 = (bf16[768]{0:T(1024)(128)(2,1)S(1)}, bf16[1792]{0:T(1024)(128)(2,1)S(1)}, bf16[1536]{0:T(1024)(128)(2,1)S(1)}) all-reduce(bf16[768]{0:T(1024)(128)(2,1)S(1)} %dynamic-update-slice, bf16[1792]{0:T(1024)(128)(2,1)S(1)} %dynamic-update-slice.1, ...), channel_id=1, replica_groups=mesh['rep'=2,'shard'=16] {'shard'}, use_global_device_ids=true, to_apply=%add.11 | all-reduce | flops 4096 | bytes 16384
  205.8 35.7 %all-gather = bf16[16,112,4]{1,2,0:T(4,128)(2,1)S(1)} all-gather(bf16[1,112,4]{1,2,0:T(4,128)(2,1)S(1)} %bitcast.455), channel_id=1, replica_groups=mesh['rep'=2,'shard'=16] {'shard'}, dimensions={0}, use_global_device_ids=true | all-gather | bytes 15232 | tf_op jit(solution)/shard_map/all_gather | solution.py:251
  248.1 11.4 fusion.140
  263.3 10.1 fusion.136
  297.2 182.0 %while.40 = (s32[]{:T(128)}, f32[24,64,128]{2,1,0:T(8,128)S(1)}, f32[4,256,24,64]{1,0,3,2:T(4,128)}, f32[4,24,64,128]{3,2,1,0:T(8,128)}, f32[4,256,24]{1,2,0:T(8...) while((s32[]{:T(128)}, f32[24,64,128]{2,1,0:T(8,128)S(1)}, ...), condition=%wide.region_5.7_spmd.clone, body=%wide.region_2.0_spmd.clone.sunk | while | flops 432687168 | bytes 17880888 | solution.py:153
  305.7 34.5 %dynamic_update_slice.73 = f32[4,256,24,64]{1,0,3,2:T(4,128)} dynamic-update-slice(f32[4,256,24,64]{1,0,3,2:T(4,128)} %get-tuple-element.896, f32[1,256,24,64]{1,0,3,2:T(1,128)S(1)} %copy.355, s32[]{:T(128)} %get-tuple-element.894, s32[]{:T(128)} %constant.126.clone.1..sunk, s32[]{:T(128)} %constant.126.clone.1..sunk, s32[]{:T(128)} %constant.126.clone.1..sunk) | dynamic-update-slice | bytes 3145732 | tf_op jit(solution)/shard_map/while/body/jit(dynamic_update_index_in_dim)/dynamic_update_slice | solution.py:153
  351.2 34.5 %dynamic_update_slice.73 = f32[4,256,24,64]{1,0,3,2:T(4,128)} dynamic-update-slice(f32[4,256,24,64]{1,0,3,2:T(4,128)} %get-tuple-element.896, f32[1,256,24,64]{1,0,3,2:T(1,128)S(1)} %copy.355, s32[]{:T(128)} %get-tuple-element.894, s32[]{:T(128)} %constant.126.clone.1..sunk, s32[]{:T(128)} %constant.126.clone.1..sunk, s32[]{:T(128)} %constant.126.clone.1..sunk) | dynamic-update-slice | bytes 3145732 | tf_op jit(solution)/shard_map/while/body/jit(dynamic_update_index_in_dim)/dynamic_update_slice | solution.py:153
  396.6 34.5 %dynamic_update_slice.73 = f32[4,256,24,64]{1,0,3,2:T(4,128)} dynamic-update-slice(f32[4,256,24,64]{1,0,3,2:T(4,128)} %get-tuple-element.896, f32[1,256,24,64]{1,0,3,2:T(1,128)S(1)} %copy.355, s32[]{:T(128)} %get-tuple-element.894, s32[]{:T(128)} %constant.126.clone.1..sunk, s32[]{:T(128)} %constant.126.clone.1..sunk, s32[]{:T(128)} %constant.126.clone.1..sunk) | dynamic-update-slice | bytes 3145732 | tf_op jit(solution)/shard_map/while/body/jit(dynamic_update_index_in_dim)/dynamic_update_slice | solution.py:153
  442.1 34.5 %dynamic_update_slice.73 = f32[4,256,24,64]{1,0,3,2:T(4,128)} dynamic-update-slice(f32[4,256,24,64]{1,0,3,2:T(4,128)} %get-tuple-element.896, f32[1,256,24,64]{1,0,3,2:T(1,128)S(1)} %copy.355, s32[]{:T(128)} %get-tuple-element.894, s32[]{:T(128)} %constant.126.clone.1..sunk, s32[]{:T(128)} %constant.126.clone.1..sunk, s32[]{:T(128)} %constant.126.clone.1..sunk) | dynamic-update-slice | bytes 3145732 | tf_op jit(solution)/shard_map/while/body/jit(dynamic_update_index_in_dim)/dynamic_update_slice | solution.py:153
  483.6 8.3 multiply_reduce_fusion.9
  499.0 7.8 multiply_reduce_fusion.6
  506.9 14.3 %multiply_reduce_fusion.7 = (f32[1536]{0:T(1024)}, f32[1024,1536]{0,1:T(8,128)}, bf16[1024,1536]{0,1:T(8,128)(2,1)}) fusion(f32[1024,1792]{0,1:T(8,128)} %copy-done.2, f32[1024,3352]{0,1:T(8,128)} %fusion.140, f32[1024,1536]{0,1:T(8,128)S(1)} %copy-done.8, f32[1024]{0:T(1024)S(1)} %multiply_multiply_fusion.1, f32[1024]{0:T(1024)S(1)} %fusion.127, ...), kind=kLoop, calls=%fused_computation.179 | loop fusion | flops 34601472 | bytes 40921088 | tf_op jit(solution)/shard_map/transpose(jvp())/reduce_sum | solution.py:52
  521.2 8.1 reshape.419
  536.4 292.3 %while.41 = (s32[]{:T(128)}, f32[24,64,128]{2,1,0:T(8,128)S(1)}, f32[4,256,24,64]{1,0,3,2:T(4,128)}, f32[4,256,128]{2,1,0:T(8,128)}, f32[4,256,128]{2,1,0:T(8,12...) while((s32[]{:T(128)}, f32[24,64,128]{2,1,0:T(8,128)S(1)}, ...), condition=%wide.region_21.23_spmd.clone, body=%wide.region_8.22_spmd.clone.sunk | while | flops 998139968 | bytes 33770432 | solution.py:177
  562.6 34.8 %dynamic_update_slice.76 = f32[4,256,24,64]{1,0,3,2:T(4,128)} dynamic-update-slice(f32[4,256,24,64]{1,0,3,2:T(4,128)} %get-tuple-element.938, f32[1,256,24,64]{1,0,3,2:T(1,128)} %copy.368, s32[]{:T(128)S(6)} %sub.232, s32[]{:T(128)} %constant.126.clone.1..sunk.1, s32[]{:T(128)} %constant.126.clone.1..sunk.1, s32[]{:T(128)} %constant.126.clone.1..sunk.1) | dynamic-update-slice | bytes 3145732 | tf_op jit(solution)/shard_map/while/body/jit(dynamic_update_index_in_dim)/dynamic_update_slice | solution.py:153
  635.7 34.7 %dynamic_update_slice.76 = f32[4,256,24,64]{1,0,3,2:T(4,128)} dynamic-update-slice(f32[4,256,24,64]{1,0,3,2:T(4,128)} %get-tuple-element.938, f32[1,256,24,64]{1,0,3,2:T(1,128)} %copy.368, s32[]{:T(128)S(6)} %sub.232, s32[]{:T(128)} %constant.126.clone.1..sunk.1, s32[]{:T(128)} %constant.126.clone.1..sunk.1, s32[]{:T(128)} %constant.126.clone.1..sunk.1) | dynamic-update-slice | bytes 3145732 | tf_op jit(solution)/shard_map/while/body/jit(dynamic_update_index_in_dim)/dynamic_update_slice | solution.py:153
  708.7 34.7 %dynamic_update_slice.76 = f32[4,256,24,64]{1,0,3,2:T(4,128)} dynamic-update-slice(f32[4,256,24,64]{1,0,3,2:T(4,128)} %get-tuple-element.938, f32[1,256,24,64]{1,0,3,2:T(1,128)} %copy.368, s32[]{:T(128)S(6)} %sub.232, s32[]{:T(128)} %constant.126.clone.1..sunk.1, s32[]{:T(128)} %constant.126.clone.1..sunk.1, s32[]{:T(128)} %constant.126.clone.1..sunk.1) | dynamic-update-slice | bytes 3145732 | tf_op jit(solution)/shard_map/while/body/jit(dynamic_update_index_in_dim)/dynamic_update_slice | solution.py:153
  781.7 34.7 %dynamic_update_slice.76 = f32[4,256,24,64]{1,0,3,2:T(4,128)} dynamic-update-slice(f32[4,256,24,64]{1,0,3,2:T(4,128)} %get-tuple-element.938, f32[1,256,24,64]{1,0,3,2:T(1,128)} %copy.368, s32[]{:T(128)S(6)} %sub.232, s32[]{:T(128)} %constant.126.clone.1..sunk.1, s32[]{:T(128)} %constant.126.clone.1..sunk.1, s32[]{:T(128)} %constant.126.clone.1..sunk.1) | dynamic-update-slice | bytes 3145732 | tf_op jit(solution)/shard_map/while/body/jit(dynamic_update_index_in_dim)/dynamic_update_slice | solution.py:153
  830.6 7.0 copy.282
  844.6 19.0 %multiply_reduce_fusion.4 = (f32[1792]{0:T(1024)S(1)}, f32[1792]{0:T(1024)S(1)}, f32[1792]{0:T(1024)S(1)}, f32[1792]{0:T(1024)S(1)}, f32[1792]{0:T(1024)S(1)}, /*index=5*/f32[1024,1792]{0,1:T(8,128)S(1)}) fusion(f32[1024,1792]{0,1:T(8,128)} %copy-done.3, f32[1024,3352]{0,1:T(8,128)} %fusion.140, f32[1024,1792]{0,1:T(8,128)} %get-tuple-element.668, ...), kind=kLoop, calls=%fused_computation.169 | loop fusion | flops 36691200 | bytes 36736000 | tf_op jit(solution)/shard_map/transpose(jvp())/reduce_sum | solution.py:42
  863.6 8.5 broadcast_multiply_fusion
  872.1 12.1 fusion.103
  884.3 12.9 %fusion.119 = f32[768,3352]{1,0:T(8,128)} fusion(bf16[1024,768]{1,0:T(8,128)(2,1)S(1)} %copy-done.11, bf16[1024,24]{0,1:T(8,128)(2,1)S(1)} %get-tuple-element.662, bf16[1024,1792]{0,1:T(8,128)(2,1)} %fusion.103, bf16[1024,1536]{0,1:T(8,128)(2,1)} %get-tuple-element.685), kind=kOutput, calls=%fused_computation.210 | convolution fusion | flops 5292834816 | bytes 18735104 | tf_op jit(solution)/shard_map/ti,tj->ij/dot_general | solution.py:199
  909.6 11.7 reduce.22
  926.4 10.7 fusion.114
  943.6 11.5 reduce.21
  956.5 20.8 %all-to-all-done.1 = bf16[16,2,24576]{2,1,0:T(2,128)(2,1)S(1)} async-done(((bf16[16,2,24576]{2,1,0:T(2,128)(2,1)}), bf16[16,2,24576]{2,1,0:T(2,128)(2,1)S(1)}, u32[]{:S(2)}, u32[]{:S(2)}) %all-to-all-start.1) | async-done | bytes 1572896 | tf_op jit(solution)/shard_map/all_to_all | solution.py:278
  977.2 27.4 %all-to-all-start.3 = ((bf16[16,2,24576]{2,1,0:T(2,128)(2,1)}), bf16[16,2,24576]{2,1,0:T(2,128)(2,1)S(1)}, u32[]{:S(2)}, u32[]{:S(2)}) async-start(bf16[16,2,24576]{2,1,0:T(2,128)(2,1)} %reshape.519), calls=%async_computation.3 | async-start | bytes 3145728 | tf_op jit(solution)/shard_map/all_to_all | solution.py:279
  1008.1 122.2 %reduce-scatter.6.cloned.1.call-done = f32[48,3352]{1,0:T(8,128)} async-done(((f32[768,3352]{1,0:T(8,128)}), f32[48,3352]{1,0:T(8,128)}) %reduce-scatter.6.cloned.1.call-update) | async-done | bytes 643600 | tf_op jit(solution)/shard_map/reduce_scatter | solution.py:296
  1130.6 40.0 %all-reduce.17 = (f32[24]{0:T(128)}, f32[24]{0:T(128)}, f32[24]{0:T(128)}) all-reduce(f32[24]{0:T(128)S(1)} %get-tuple-element.661, f32[24]{0:T(128)S(1)} %negate_multiply_fusion, f32[24]{0:T(128)S(1)} %reduce_sum.344), channel_id=1, replica_groups=mesh['rep'=2,'shard'=16] {'rep','shard'}, use_global_device_ids=true, to_apply=%region_38.40 | all-reduce | flops 72 | bytes 576 | tf_op jit(solution)/shard_map/psum | solution.py:302
  1170.6 75.7 %all-reduce.18 = (f32[768]{0:T(1024)S(1)}, f32[1792]{0:T(1024)S(1)}, f32[1536]{0:T(1024)S(1)}) all-reduce(f32[768]{0:T(1024)S(1)} %get-tuple-element.592, f32[1792]{0:T(1024)S(1)} %get-tuple-element.590, f32[1536]{0:T(1024)S(1)} %copy-done.36), channel_id=2, replica_groups=mesh['rep'=2,'shard'=16] {'shard'}, use_global_device_ids=true, to_apply=%region_25.27.clone | all-reduce | flops 4096 | bytes 32768
  (432 shorter events, 332.5 us)
Async XLA Ops:
  7.2 240.9 %all-gather.4.cloned.1.call-start = ((), (), s32[]{:S(2)}) async-start(), calls=%async_computation.7 | async-start | bytes 5640192 | tf_op jit(solution)/shard_map/all_gather | solution.py:250
  12.6 73.9 %copy-start.41 = (u32[32]{0:T(128)S(1)}, u32[32]{0:T(128)}, u32[]{:S(2)}) copy-start(u32[32]{0:T(128)} %constant.162) | copy-start | bytes 388
  12.6 76.5 %copy-start.44 = (bf16[112]{0:T(256)(128)(2,1)S(1)}, bf16[112]{0:T(256)(128)(2,1)}, u32[]{:S(2)}) copy-start(bf16[112]{0:T(256)(128)(2,1)} %param.26) | copy-start | bytes 676
  12.6 76.7 %copy-start.45 = (bf16[96]{0:T(256)(128)(2,1)S(1)}, bf16[96]{0:T(256)(128)(2,1)}, u32[]{:S(2)}) copy-start(bf16[96]{0:T(256)(128)(2,1)} %param.30) | copy-start | bytes 580
  12.6 77.0 %copy-start.46 = (bf16[48]{0:T(256)(128)(2,1)S(1)}, bf16[48]{0:T(256)(128)(2,1)}, u32[]{:S(2)}) copy-start(bf16[48]{0:T(256)(128)(2,1)} %param.23) | copy-start | bytes 292
  12.6 193.1 %copy-start.42 = (bf16[112,4]{0,1:T(4,128)(2,1)S(1)}, bf16[112,4]{0,1:T(4,128)(2,1)}, u32[]{:S(2)}) copy-start(bf16[112,4]{0,1:T(4,128)(2,1)} %param.25) | copy-start | bytes 2692
  12.6 228.9 %copy-start.43 = (f32[24]{0:T(128)S(1)}, f32[24]{0:T(128)}, u32[]{:S(2)}) copy-start(f32[24]{0:T(128)} %param.29) | copy-start | bytes 292
  12.7 229.0 %copy-start.47 = (s32[1,16]{1,0:T(1,128)S(1)}, s32[1,16]{1,0:T(1,128)}, u32[]{:S(2)}) copy-start(s32[1,16]{1,0:T(1,128)} %param.21) | copy-start | bytes 196
  12.7 230.4 %copy-start.49 = (f32[24]{0:T(128)S(1)}, f32[24]{0:T(128)}, u32[]{:S(2)}) copy-start(f32[24]{0:T(128)} %param.28) | copy-start | bytes 292
  81.1 178.3 %copy-start.5 = (bf16[16,1,64,768]{3,2,1,0:T(8,128)(2,1)}, bf16[16,1,64,768]{3,2,1,0:T(8,128)(2,1)S(1)}, u32[]{:S(2)}) copy-start(bf16[16,1,64,768]{3,2,1,0:T(8,128)(2,1)S(1)} %all_to_all.42) | copy-start | bytes 4718596
  81.1 164.1 %all-to-all-start.2 = ((bf16[16,1,64,768]{3,2,1,0:T(8,128)(2,1)}), bf16[16,1,64,768]{3,2,1,0:T(8,128)(2,1)}, u32[]{:S(2)}, u32[]{:S(2)}) async-start(bf16[16,1,64,768]{3,2,1,0:T(8,128)(2,1)} %get-tuple-element.697), calls=%async_computation.2 | async-start | bytes 3145728 | tf_op jit(solution)/shard_map/all_to_all | solution.py:244
  85.6 413.4 %all-gather.6.cloned.1.call-start = ((), (), s32[]{:S(2)}) async-start(), calls=%async_computation.8 | async-start | bytes 2506752 | tf_op jit(solution)/shard_map/all_gather | solution.py:254
  86.4 921.7 %reduce-scatter.8.cloned.1.call-start = ((), (), s32[]{:S(2)}) async-start(), calls=%async_computation.10 | async-start | bytes 5013504 | tf_op jit(solution)/shard_map/reduce_scatter | solution.py:300
  205.8 53.7 %copy-start.23 = (f32[768]{0:T(1024)}, f32[768]{0:T(1024)S(1)}, u32[]{:S(2)}) copy-start(f32[768]{0:T(1024)S(1)} %convert_element_type.160) | copy-start | bytes 9220
  241.7 265.1 %copy-start.29 = (f32[1536]{0:T(1024)}, f32[1536]{0:T(1024)S(1)}, u32[]{:S(2)}) copy-start(f32[1536]{0:T(1024)S(1)} %convert_element_type.165) | copy-start | bytes 18436
  243.0 20.2 %copy-start.15 = (f32[1792]{0:T(1024)}, f32[1792]{0:T(1024)S(1)}, u32[]{:S(2)}) copy-start(f32[1792]{0:T(1024)S(1)} %get-tuple-element.594) | copy-start | bytes 21508
  243.1 20.2 %copy-start.17 = (f32[1792]{0:T(1024)}, f32[1792]{0:T(1024)S(1)}, u32[]{:S(2)}) copy-start(f32[1792]{0:T(1024)S(1)} %get-tuple-element.595) | copy-start | bytes 21508
  243.1 20.2 %copy-start.19 = (f32[1792]{0:T(1024)}, f32[1792]{0:T(1024)S(1)}, u32[]{:S(2)}) copy-start(f32[1792]{0:T(1024)S(1)} %get-tuple-element.596) | copy-start | bytes 21508
  243.1 20.2 %copy-start.21 = (f32[1792]{0:T(1024)}, f32[1792]{0:T(1024)S(1)}, u32[]{:S(2)}) copy-start(f32[1792]{0:T(1024)S(1)} %get-tuple-element.597) | copy-start | bytes 21508
  243.1 47.7 %copy-start.39 = (f32[24]{0:T(128)}, f32[24]{0:T(128)S(1)}, u32[]{:S(2)}) copy-start(f32[24]{0:T(128)S(1)} %exponential_negate_fusion) | copy-start | bytes 292
  529.3 601.0 %reduce-scatter.6.cloned.1.call-start = ((), (), s32[]{:S(2)}) async-start(), calls=%async_computation.9 | async-start | bytes 11280384 | tf_op jit(solution)/shard_map/reduce_scatter | solution.py:296
  844.5 19.0 %copy-start.16 = (f32[1792]{0:T(1024)S(1)}, f32[1792]{0:T(1024)}, u32[]{:S(2)}) copy-start(f32[1792]{0:T(1024)} %copy-done.15) | copy-start | bytes 21508
  844.5 19.0 %copy-start.18 = (f32[1792]{0:T(1024)S(1)}, f32[1792]{0:T(1024)}, u32[]{:S(2)}) copy-start(f32[1792]{0:T(1024)} %copy-done.17) | copy-start | bytes 21508
  844.6 19.0 %copy-start.20 = (f32[1792]{0:T(1024)S(1)}, f32[1792]{0:T(1024)}, u32[]{:S(2)}) copy-start(f32[1792]{0:T(1024)} %copy-done.19) | copy-start | bytes 21508
  922.6 54.6 %all-to-all-start.1 = ((bf16[16,2,24576]{2,1,0:T(2,128)(2,1)}), bf16[16,2,24576]{2,1,0:T(2,128)(2,1)S(1)}, u32[]{:S(2)}, u32[]{:S(2)}) async-start(bf16[16,2,24576]{2,1,0:T(2,128)(2,1)} %reshape.517), calls=%async_computation.1 | async-start | bytes 3145728 | tf_op jit(solution)/shard_map/all_to_all | solution.py:278
  943.6 62.5 %copy-start.48 = (s32[1,16]{1,0:T(1,128)S(1)}, s32[1,16]{1,0:T(1,128)}, u32[]{:S(2)}) copy-start(s32[1,16]{1,0:T(1,128)} %param.22) | copy-start | bytes 196
  943.6 186.8 %copy-start.31 = (f32[1536]{0:T(1024)S(1)}, f32[1536]{0:T(1024)}, u32[]{:S(2)}) copy-start(f32[1536]{0:T(1024)} %get-tuple-element.659) | copy-start | bytes 18436
  943.6 187.0 %copy-start.50 = (f32[24]{0:T(128)S(1)}, f32[24]{0:T(128)}, u32[]{:S(2)}) copy-start(f32[24]{0:T(128)} %param.28) | copy-start | bytes 292
  943.6 227.0 %copy-start.36 = (f32[1536]{0:T(1024)S(1)}, f32[1536]{0:T(1024)}, u32[]{:S(2)}) copy-start(f32[1536]{0:T(1024)} %get-tuple-element.588) | copy-start | bytes 18436
  977.2 281.6 %all-to-all-start.3 = ((bf16[16,2,24576]{2,1,0:T(2,128)(2,1)}), bf16[16,2,24576]{2,1,0:T(2,128)(2,1)S(1)}, u32[]{:S(2)}, u32[]{:S(2)}) async-start(bf16[16,2,24576]{2,1,0:T(2,128)(2,1)} %reshape.519), calls=%async_computation.3 | async-start | bytes 3145728 | tf_op jit(solution)/shard_map/all_to_all | solution.py:279
  1004.6 241.9 %reduce-scatter.10.cloned.1.call-start = ((), (), s32[]{:S(2)}) async-start(), calls=%async_computation.11 | async-start | bytes 974848
  1006.1 269.6 %all-reduce.24.cloned.1.call-start = ((), (), s32[]{:S(2)}) async-start(), calls=%async_computation.12 | async-start | bytes 1916928 | tf_op jit(solution)/shard_map/psum | solution.py:283
  (28 other events, 250.3 us)
Sparse Core Ops, SparseCore 0:
  10.8 132.4 all-gather.3
  146.1 62.0 all-gather.5
  529.4 135.1 reduce-scatter.7
  897.3 232.9 reduce-scatter.5
  1133.0 76.8 reduce-scatter.9
  1212.3 15.8 all-reduce.23
where the time goes:
time: 1300 us; the launch traced here: 1290 us
  local copies, waits for them, and re-layouts  440 us (34%)
  blocking collectives  336 us (26%)
  matrix products  164 us (13%)
  other arithmetic  146 us (11%)
  waiting for transfers between devices  144 us (11%)
  starting transfers between devices  35.8 us (3%)
  between operations  19.1 us (1%)
    dynamic_update_slice x16, local copies, waits for them, and re-layouts, forward_seq(): final_state, kept = lax.scan(block_forward, start, blocks)  295 us
    unnamed x2, blocking collectives  192 us
    reduce_scatter x1, waiting for transfers between devices, on_device(): lax.psum_scatter(summed[1], 'shard', scatter_dimension=0, tiled=True)  122 us
    all_to_all x1, blocking collectives, on_device(): lax.all_to_all(sent_tokens, 'shard', split_axis=0, concat_axis=2, tiled=T...  65.5 us
    unnamed x131, local copies, waits for them, and re-layouts  55.2 us
    psum x1, blocking collectives, on_device(): lax.psum((head_terms[0], head_terms[1], head_terms[2]), ('rep', 'shard'))  40 us
    another operation x34, other arithmetic  37.8 us
    all_gather x1, blocking collectives, on_device(): lax.all_gather(conv_weight, 'shard', axis=0, tiled=True)  35.7 us
  transfers between devices with their start and end apart: 9, of which 2 were waited for; matrix products, arithmetic and copies ran while one was open for 55% of the time, Pallas kernels for 0%

commit v1 on v0

--- a/solution.py
+++ b/solution.py
@@ -240,7 +240,12 @@
     sent_tokens = jnp.take(tokens, inverse, axis=0).reshape(peers, 1, piece, width)
     sent_cot = jnp.take(cotangent, inverse, axis=0).reshape(peers, 1, piece, width)
     got_tokens, got_cot = (
-        lax.all_to_all(sent_tokens, "shard", split_axis=0, concat_axis=2, tiled=True),
+        jnp.concatenate(
+            lax.all_to_all(
+                jnp.stack(jnp.split(sent_tokens, lax.axis_size("shard"), axis=0)), "shard", 0, 0
+            ),
+            axis=2,
+        ),
         lax.all_to_all(sent_cot, "shard", split_axis=0, concat_axis=2, tiled=True),
     )
     seq_len = got_tokens.shape[2]

time: 1300 us -> 1300 us (level)
    unnamed x131 -> x149, local copies, waits for them, and re-layouts: 55.2 us -> 54.7 us
where the time goes in v1:
time: 1300 us; the launch traced here: 1290 us
  local copies, waits for them, and re-layouts  441 us (34%)
  blocking collectives  337 us (26%)
  matrix products  163 us (13%)
  other arithmetic  146 us (11%)
  waiting for transfers between devices  145 us (11%)
  starting transfers between devices  37 us (3%)
  between operations  19.3 us (1%)
    dynamic_update_slice x16, local copies, waits for them, and re-layouts, forward_seq(): final_state, kept = lax.scan(block_forward, start, blocks)  295 us
    unnamed x2, blocking collectives  192 us
    reduce_scatter x1, waiting for transfers between devices, on_device(): lax.psum_scatter(summed[1], 'shard', scatter_dimension=0, tiled=True)  123 us
    all_to_all x1, blocking collectives, on_device(): lax.all_to_all(jnp.stack(jnp.split(sent_tokens, lax.axis_size('shard'), a...  66.4 us
    unnamed x149, local copies, waits for them, and re-layouts  54.7 us
    psum x1, blocking collectives, on_device(): lax.psum((head_terms[0], head_terms[1], head_terms[2]), ('rep', 'shard'))  40.1 us
    another operation x34, other arithmetic  37.8 us
    all_gather x1, blocking collectives, on_device(): lax.all_gather(conv_weight, 'shard', axis=0, tiled=True)  35.7 us
  transfers between devices with their start and end apart: 9, of which 2 were waited for; matrix products, arithmetic and copies ran while one was open for 55% of the time, Pallas kernels for 0%

profile of v1, /device:TPU:0, one launch (start us, length us, event | category | flops | bytes accessed | tf_op | source)
XLA Modules:
  0.0 1289.6 jit_solution(7078022193060803589)
XLA Ops:
  14.5 66.4 %all_to_all.38 = bf16[16,1,1,64,768]{4,3,2,1,0:T(8,128)(2,1)S(1)} all-to-all(bf16[16,1,1,64,768]{4,3,2,1,0:T(8,128)(2,1)S(1)} %fusion.126), channel_id=1, replica_groups=mesh['rep'=2,'shard'=16] {'shard'}, dimensions={0} | all-to-all | bytes 3145728 | tf_op jit(solution)/shard_map/all_to_all | solution.py:244
  89.8 116.5 %all-reduce.21 = (bf16[768]{0:T(1024)(128)(2,1)S(1)}, bf16[1792]{0:T(1024)(128)(2,1)S(1)}, bf16[1536]{0:T(1024)(128)(2,1)S(1)}) all-reduce(bf16[768]{0:T(1024)(128)(2,1)S(1)} %dynamic-update-slice, bf16[1792]{0:T(1024)(128)(2,1)S(1)} %dynamic-update-slice.1, ...), channel_id=1, replica_groups=mesh['rep'=2,'shard'=16] {'shard'}, use_global_device_ids=true, to_apply=%add.11 | all-reduce | flops 4096 | bytes 16384
  206.4 35.7 %all-gather = bf16[16,112,4]{1,2,0:T(4,128)(2,1)S(1)} all-gather(bf16[1,112,4]{1,2,0:T(4,128)(2,1)S(1)} %bitcast.521), channel_id=1, replica_groups=mesh['rep'=2,'shard'=16] {'shard'}, dimensions={0}, use_global_device_ids=true | all-gather | bytes 15232 | tf_op jit(solution)/shard_map/all_gather | solution.py:256
  248.8 11.1 fusion.156
  263.8 10.1 fusion.152
  297.7 182.0 %while.40 = (s32[]{:T(128)}, f32[24,64,128]{2,1,0:T(8,128)S(1)}, f32[4,256,24,64]{1,0,3,2:T(4,128)}, f32[4,24,64,128]{3,2,1,0:T(8,128)}, f32[4,256,24]{1,2,0:T(8...) while((s32[]{:T(128)}, f32[24,64,128]{2,1,0:T(8,128)S(1)}, ...), condition=%wide.region_5.7_spmd.clone, body=%wide.region_2.0_spmd.clone.sunk | while | flops 432687168 | bytes 17880888 | solution.py:153
  306.2 34.5 %dynamic_update_slice.73 = f32[4,256,24,64]{1,0,3,2:T(4,128)} dynamic-update-slice(f32[4,256,24,64]{1,0,3,2:T(4,128)} %get-tuple-element.896, f32[1,256,24,64]{1,0,3,2:T(1,128)S(1)} %copy.357, s32[]{:T(128)} %get-tuple-element.894, s32[]{:T(128)} %constant.126.clone.1..sunk, s32[]{:T(128)} %constant.126.clone.1..sunk, s32[]{:T(128)} %constant.126.clone.1..sunk) | dynamic-update-slice | bytes 3145732 | tf_op jit(solution)/shard_map/while/body/jit(dynamic_update_index_in_dim)/dynamic_update_slice | solution.py:153
  351.7 34.5 %dynamic_update_slice.73 = f32[4,256,24,64]{1,0,3,2:T(4,128)} dynamic-update-slice(f32[4,256,24,64]{1,0,3,2:T(4,128)} %get-tuple-element.896, f32[1,256,24,64]{1,0,3,2:T(1,128)S(1)} %copy.357, s32[]{:T(128)} %get-tuple-element.894, s32[]{:T(128)} %constant.126.clone.1..sunk, s32[]{:T(128)} %constant.126.clone.1..sunk, s32[]{:T(128)} %constant.126.clone.1..sunk) | dynamic-update-slice | bytes 3145732 | tf_op jit(solution)/shard_map/while/body/jit(dynamic_update_index_in_dim)/dynamic_update_slice | solution.py:153
  397.1 34.5 %dynamic_update_slice.73 = f32[4,256,24,64]{1,0,3,2:T(4,128)} dynamic-update-slice(f32[4,256,24,64]{1,0,3,2:T(4,128)} %get-tuple-element.896, f32[1,256,24,64]{1,0,3,2:T(1,128)S(1)} %copy.357, s32[]{:T(128)} %get-tuple-element.894, s32[]{:T(128)} %constant.126.clone.1..sunk, s32[]{:T(128)} %constant.126.clone.1..sunk, s32[]{:T(128)} %constant.126.clone.1..sunk) | dynamic-update-slice | bytes 3145732 | tf_op jit(solution)/shard_map/while/body/jit(dynamic_update_index_in_dim)/dynamic_update_slice | solution.py:153
  442.6 34.5 %dynamic_update_slice.73 = f32[4,256,24,64]{1,0,3,2:T(4,128)} dynamic-update-slice(f32[4,256,24,64]{1,0,3,2:T(4,128)} %get-tuple-element.896, f32[1,256,24,64]{1,0,3,2:T(1,128)S(1)} %copy.357, s32[]{:T(128)} %get-tuple-element.894, s32[]{:T(128)} %constant.126.clone.1..sunk, s32[]{:T(128)} %constant.126.clone.1..sunk, s32[]{:T(128)} %constant.126.clone.1..sunk) | dynamic-update-slice | bytes 3145732 | tf_op jit(solution)/shard_map/while/body/jit(dynamic_update_index_in_dim)/dynamic_update_slice | solution.py:153
  484.1 8.3 multiply_reduce_fusion.9
  499.5 7.8 multiply_reduce_fusion.6
  507.4 14.3 %multiply_reduce_fusion.7 = (f32[1536]{0:T(1024)}, f32[1024,1536]{0,1:T(8,128)}, bf16[1024,1536]{0,1:T(8,128)(2,1)}) fusion(f32[1024,1792]{0,1:T(8,128)} %copy-done.2, f32[1024,3352]{0,1:T(8,128)} %fusion.156, f32[1024,1536]{0,1:T(8,128)S(1)} %copy-done.8, f32[1024]{0:T(1024)S(1)} %multiply_multiply_fusion.1, f32[1024]{0:T(1024)S(1)} %fusion.143, ...), kind=kLoop, calls=%fused_computation.179 | loop fusion | flops 34601472 | bytes 40921088 | tf_op jit(solution)/shard_map/transpose(jvp())/reduce_sum | solution.py:52
  521.7 8.1 reshape.440
  536.9 292.3 %while.41 = (s32[]{:T(128)}, f32[24,64,128]{2,1,0:T(8,128)S(1)}, f32[4,256,24,64]{1,0,3,2:T(4,128)}, f32[4,256,128]{2,1,0:T(8,128)}, f32[4,256,128]{2,1,0:T(8,12...) while((s32[]{:T(128)}, f32[24,64,128]{2,1,0:T(8,128)S(1)}, ...), condition=%wide.region_21.23_spmd.clone, body=%wide.region_8.22_spmd.clone.sunk | while | flops 998139968 | bytes 33770432 | solution.py:177
  563.1 34.8 %dynamic_update_slice.76 = f32[4,256,24,64]{1,0,3,2:T(4,128)} dynamic-update-slice(f32[4,256,24,64]{1,0,3,2:T(4,128)} %get-tuple-element.938, f32[1,256,24,64]{1,0,3,2:T(1,128)} %copy.370, s32[]{:T(128)S(6)} %sub.232, s32[]{:T(128)} %constant.126.clone.1..sunk.1, s32[]{:T(128)} %constant.126.clone.1..sunk.1, s32[]{:T(128)} %constant.126.clone.1..sunk.1) | dynamic-update-slice | bytes 3145732 | tf_op jit(solution)/shard_map/while/body/jit(dynamic_update_index_in_dim)/dynamic_update_slice | solution.py:153
  636.2 34.8 %dynamic_update_slice.76 = f32[4,256,24,64]{1,0,3,2:T(4,128)} dynamic-update-slice(f32[4,256,24,64]{1,0,3,2:T(4,128)} %get-tuple-element.938, f32[1,256,24,64]{1,0,3,2:T(1,128)} %copy.370, s32[]{:T(128)S(6)} %sub.232, s32[]{:T(128)} %constant.126.clone.1..sunk.1, s32[]{:T(128)} %constant.126.clone.1..sunk.1, s32[]{:T(128)} %constant.126.clone.1..sunk.1) | dynamic-update-slice | bytes 3145732 | tf_op jit(solution)/shard_map/while/body/jit(dynamic_update_index_in_dim)/dynamic_update_slice | solution.py:153
  709.2 34.7 %dynamic_update_slice.76 = f32[4,256,24,64]{1,0,3,2:T(4,128)} dynamic-update-slice(f32[4,256,24,64]{1,0,3,2:T(4,128)} %get-tuple-element.938, f32[1,256,24,64]{1,0,3,2:T(1,128)} %copy.370, s32[]{:T(128)S(6)} %sub.232, s32[]{:T(128)} %constant.126.clone.1..sunk.1, s32[]{:T(128)} %constant.126.clone.1..sunk.1, s32[]{:T(128)} %constant.126.clone.1..sunk.1) | dynamic-update-slice | bytes 3145732 | tf_op jit(solution)/shard_map/while/body/jit(dynamic_update_index_in_dim)/dynamic_update_slice | solution.py:153
  782.2 34.7 %dynamic_update_slice.76 = f32[4,256,24,64]{1,0,3,2:T(4,128)} dynamic-update-slice(f32[4,256,24,64]{1,0,3,2:T(4,128)} %get-tuple-element.938, f32[1,256,24,64]{1,0,3,2:T(1,128)} %copy.370, s32[]{:T(128)S(6)} %sub.232, s32[]{:T(128)} %constant.126.clone.1..sunk.1, s32[]{:T(128)} %constant.126.clone.1..sunk.1, s32[]{:T(128)} %constant.126.clone.1..sunk.1) | dynamic-update-slice | bytes 3145732 | tf_op jit(solution)/shard_map/while/body/jit(dynamic_update_index_in_dim)/dynamic_update_slice | solution.py:153
  831.1 7.0 copy.282
  845.1 19.0 %multiply_reduce_fusion.4 = (f32[1792]{0:T(1024)S(1)}, f32[1792]{0:T(1024)S(1)}, f32[1792]{0:T(1024)S(1)}, f32[1792]{0:T(1024)S(1)}, f32[1792]{0:T(1024)S(1)}, /*index=5*/f32[1024,1792]{0,1:T(8,128)S(1)}) fusion(f32[1024,1792]{0,1:T(8,128)} %copy-done.3, f32[1024,3352]{0,1:T(8,128)} %fusion.156, f32[1024,1792]{0,1:T(8,128)} %get-tuple-element.668, ...), kind=kLoop, calls=%fused_computation.169 | loop fusion | flops 36691200 | bytes 36736000 | tf_op jit(solution)/shard_map/transpose(jvp())/reduce_sum | solution.py:42
  864.1 8.5 broadcast_multiply_fusion
  872.6 12.1 fusion.103
  884.8 12.9 %fusion.119 = f32[768,3352]{1,0:T(8,128)} fusion(bf16[1024,768]{1,0:T(8,128)(2,1)S(1)} %copy-done.13, bf16[1024,24]{0,1:T(8,128)(2,1)S(1)} %get-tuple-element.662, bf16[1024,1792]{0,1:T(8,128)(2,1)} %fusion.103, bf16[1024,1536]{0,1:T(8,128)(2,1)} %get-tuple-element.685), kind=kOutput, calls=%fused_computation.210 | convolution fusion | flops 5292834816 | bytes 18735104 | tf_op jit(solution)/shard_map/ti,tj->ij/dot_general | solution.py:199
  910.1 11.7 reduce.21
  926.9 10.7 fusion.114
  944.1 11.4 reduce.20
  956.9 20.6 %all-to-all-done.1 = bf16[16,2,24576]{2,1,0:T(2,128)(2,1)S(1)} async-done(((bf16[16,2,24576]{2,1,0:T(2,128)(2,1)}), bf16[16,2,24576]{2,1,0:T(2,128)(2,1)S(1)}, u32[]{:S(2)}, u32[]{:S(2)}) %all-to-all-start.1) | async-done | bytes 1572896 | tf_op jit(solution)/shard_map/all_to_all | solution.py:283
  977.6 28.4 %all-to-all-start.3 = ((bf16[16,2,24576]{2,1,0:T(2,128)(2,1)}), bf16[16,2,24576]{2,1,0:T(2,128)(2,1)S(1)}, u32[]{:S(2)}, u32[]{:S(2)}) async-start(bf16[16,2,24576]{2,1,0:T(2,128)(2,1)} %reshape.540), calls=%async_computation.3 | async-start | bytes 3145728 | tf_op jit(solution)/shard_map/all_to_all | solution.py:284
  1007.5 122.9 %reduce-scatter.6.cloned.1.call-done = f32[48,3352]{1,0:T(8,128)} async-done(((f32[768,3352]{1,0:T(8,128)}), f32[48,3352]{1,0:T(8,128)}) %reduce-scatter.6.cloned.1.call-update) | async-done | bytes 643600 | tf_op jit(solution)/shard_map/reduce_scatter | solution.py:301
  1132.5 40.1 %all-reduce.17 = (f32[24]{0:T(128)}, f32[24]{0:T(128)}, f32[24]{0:T(128)}) all-reduce(f32[24]{0:T(128)S(1)} %get-tuple-element.661, f32[24]{0:T(128)S(1)} %negate_multiply_fusion, f32[24]{0:T(128)S(1)} %reduce_sum.344), channel_id=1, replica_groups=mesh['rep'=2,'shard'=16] {'rep','shard'}, use_global_device_ids=true, to_apply=%region_38.40 | all-reduce | flops 72 | bytes 576 | tf_op jit(solution)/shard_map/psum | solution.py:307
  1172.6 75.3 %all-reduce.18 = (f32[768]{0:T(1024)S(1)}, f32[1792]{0:T(1024)S(1)}, f32[1536]{0:T(1024)S(1)}) all-reduce(f32[768]{0:T(1024)S(1)} %get-tuple-element.592, f32[1792]{0:T(1024)S(1)} %get-tuple-element.590, f32[1536]{0:T(1024)S(1)} %copy-done.38), channel_id=2, replica_groups=mesh['rep'=2,'shard'=16] {'shard'}, use_global_device_ids=true, to_apply=%region_25.27.clone | all-reduce | flops 4096 | bytes 32768
  (452 shorter events, 333.2 us)
Async XLA Ops:
  7.2 241.6 %all-gather.4.cloned.1.call-start = ((), (), s32[]{:S(2)}) async-start(), calls=%async_computation.7 | async-start | bytes 5640192 | tf_op jit(solution)/shard_map/all_gather | solution.py:255
  14.4 72.1 %copy-start.43 = (u32[32]{0:T(128)S(1)}, u32[32]{0:T(128)}, u32[]{:S(2)}) copy-start(u32[32]{0:T(128)} %constant.162) | copy-start | bytes 388
  14.5 74.6 %copy-start.46 = (bf16[112]{0:T(256)(128)(2,1)S(1)}, bf16[112]{0:T(256)(128)(2,1)}, u32[]{:S(2)}) copy-start(bf16[112]{0:T(256)(128)(2,1)} %param.26) | copy-start | bytes 676
  14.5 74.9 %copy-start.47 = (bf16[96]{0:T(256)(128)(2,1)S(1)}, bf16[96]{0:T(256)(128)(2,1)}, u32[]{:S(2)}) copy-start(bf16[96]{0:T(256)(128)(2,1)} %param.30) | copy-start | bytes 580
  14.5 75.1 %copy-start.48 = (bf16[48]{0:T(256)(128)(2,1)S(1)}, bf16[48]{0:T(256)(128)(2,1)}, u32[]{:S(2)}) copy-start(bf16[48]{0:T(256)(128)(2,1)} %param.23) | copy-start | bytes 292
  14.5 191.9 %copy-start.44 = (bf16[112,4]{0,1:T(4,128)(2,1)S(1)}, bf16[112,4]{0,1:T(4,128)(2,1)}, u32[]{:S(2)}) copy-start(bf16[112,4]{0,1:T(4,128)(2,1)} %param.25) | copy-start | bytes 2692
  14.5 227.6 %copy-start.45 = (f32[24]{0:T(128)S(1)}, f32[24]{0:T(128)}, u32[]{:S(2)}) copy-start(f32[24]{0:T(128)} %param.29) | copy-start | bytes 292
  14.5 227.8 %copy-start.49 = (s32[1,16]{1,0:T(1,128)S(1)}, s32[1,16]{1,0:T(1,128)}, u32[]{:S(2)}) copy-start(s32[1,16]{1,0:T(1,128)} %param.21) | copy-start | bytes 196
  14.5 229.1 %copy-start.51 = (f32[24]{0:T(128)S(1)}, f32[24]{0:T(128)}, u32[]{:S(2)}) copy-start(f32[24]{0:T(128)} %param.28) | copy-start | bytes 292
  80.9 164.8 %copy-start.5 = (bf16[16,1,1,64,768]{4,3,2,1,0:T(8,128)(2,1)}, bf16[16,1,1,64,768]{4,3,2,1,0:T(8,128)(2,1)S(1)}, u32[]{:S(2)}) copy-start(bf16[16,1,1,64,768]{4,3,2,1,0:T(8,128)(2,1)S(1)} %all_to_all.38) | copy-start | bytes 4718596
  80.9 164.9 %all-to-all-start.2 = ((bf16[16,1,64,768]{3,2,1,0:T(8,128)(2,1)}), bf16[16,1,64,768]{3,2,1,0:T(8,128)(2,1)}, u32[]{:S(2)}, u32[]{:S(2)}) async-start(bf16[16,1,64,768]{3,2,1,0:T(8,128)(2,1)} %get-tuple-element.697), calls=%async_computation.2 | async-start | bytes 3145728 | tf_op jit(solution)/shard_map/all_to_all | solution.py:249
  85.6 413.9 %all-gather.6.cloned.1.call-start = ((), (), s32[]{:S(2)}) async-start(), calls=%async_computation.8 | async-start | bytes 2506752 | tf_op jit(solution)/shard_map/all_gather | solution.py:259
  86.4 921.1 %reduce-scatter.8.cloned.1.call-start = ((), (), s32[]{:S(2)}) async-start(), calls=%async_computation.10 | async-start | bytes 5013504 | tf_op jit(solution)/shard_map/reduce_scatter | solution.py:305
  206.4 42.4 %copy-start.25 = (f32[768]{0:T(1024)}, f32[768]{0:T(1024)S(1)}, u32[]{:S(2)}) copy-start(f32[768]{0:T(1024)S(1)} %convert_element_type.157) | copy-start | bytes 9220
  242.3 265.1 %copy-start.31 = (f32[1536]{0:T(1024)}, f32[1536]{0:T(1024)S(1)}, u32[]{:S(2)}) copy-start(f32[1536]{0:T(1024)S(1)} %convert_element_type.162) | copy-start | bytes 18436
  243.6 20.1 %copy-start.17 = (f32[1792]{0:T(1024)}, f32[1792]{0:T(1024)S(1)}, u32[]{:S(2)}) copy-start(f32[1792]{0:T(1024)S(1)} %get-tuple-element.594) | copy-start | bytes 21508
  243.6 20.1 %copy-start.19 = (f32[1792]{0:T(1024)}, f32[1792]{0:T(1024)S(1)}, u32[]{:S(2)}) copy-start(f32[1792]{0:T(1024)S(1)} %get-tuple-element.595) | copy-start | bytes 21508
  243.7 20.1 %copy-start.21 = (f32[1792]{0:T(1024)}, f32[1792]{0:T(1024)S(1)}, u32[]{:S(2)}) copy-start(f32[1792]{0:T(1024)S(1)} %get-tuple-element.596) | copy-start | bytes 21508
  243.7 20.1 %copy-start.23 = (f32[1792]{0:T(1024)}, f32[1792]{0:T(1024)S(1)}, u32[]{:S(2)}) copy-start(f32[1792]{0:T(1024)S(1)} %get-tuple-element.597) | copy-start | bytes 21508
  243.7 47.6 %copy-start.41 = (f32[24]{0:T(128)}, f32[24]{0:T(128)S(1)}, u32[]{:S(2)}) copy-start(f32[24]{0:T(128)S(1)} %exponential_negate_fusion) | copy-start | bytes 292
  529.8 600.5 %reduce-scatter.6.cloned.1.call-start = ((), (), s32[]{:S(2)}) async-start(), calls=%async_computation.9 | async-start | bytes 11280384 | tf_op jit(solution)/shard_map/reduce_scatter | solution.py:301
  845.0 19.0 %copy-start.18 = (f32[1792]{0:T(1024)S(1)}, f32[1792]{0:T(1024)}, u32[]{:S(2)}) copy-start(f32[1792]{0:T(1024)} %copy-done.17) | copy-start | bytes 21508
  845.0 19.0 %copy-start.20 = (f32[1792]{0:T(1024)S(1)}, f32[1792]{0:T(1024)}, u32[]{:S(2)}) copy-start(f32[1792]{0:T(1024)} %copy-done.19) | copy-start | bytes 21508
  845.1 19.0 %copy-start.22 = (f32[1792]{0:T(1024)S(1)}, f32[1792]{0:T(1024)}, u32[]{:S(2)}) copy-start(f32[1792]{0:T(1024)} %copy-done.21) | copy-start | bytes 21508
  923.1 54.4 %all-to-all-start.1 = ((bf16[16,2,24576]{2,1,0:T(2,128)(2,1)}), bf16[16,2,24576]{2,1,0:T(2,128)(2,1)S(1)}, u32[]{:S(2)}, u32[]{:S(2)}) async-start(bf16[16,2,24576]{2,1,0:T(2,128)(2,1)} %reshape.538), calls=%async_computation.1 | async-start | bytes 3145728 | tf_op jit(solution)/shard_map/all_to_all | solution.py:283
  956.9 175.4 %copy-start.50 = (s32[1,16]{1,0:T(1,128)S(1)}, s32[1,16]{1,0:T(1,128)}, u32[]{:S(2)}) copy-start(s32[1,16]{1,0:T(1,128)} %param.22) | copy-start | bytes 196
  956.9 175.4 %copy-start.33 = (f32[1536]{0:T(1024)S(1)}, f32[1536]{0:T(1024)}, u32[]{:S(2)}) copy-start(f32[1536]{0:T(1024)} %get-tuple-element.659) | copy-start | bytes 18436
  956.9 175.6 %copy-start.52 = (f32[24]{0:T(128)S(1)}, f32[24]{0:T(128)}, u32[]{:S(2)}) copy-start(f32[24]{0:T(128)} %param.28) | copy-start | bytes 292
  956.9 215.7 %copy-start.38 = (f32[1536]{0:T(1024)S(1)}, f32[1536]{0:T(1024)}, u32[]{:S(2)}) copy-start(f32[1536]{0:T(1024)} %get-tuple-element.588) | copy-start | bytes 18436
  977.6 282.9 %all-to-all-start.3 = ((bf16[16,2,24576]{2,1,0:T(2,128)(2,1)}), bf16[16,2,24576]{2,1,0:T(2,128)(2,1)S(1)}, u32[]{:S(2)}, u32[]{:S(2)}) async-start(bf16[16,2,24576]{2,1,0:T(2,128)(2,1)} %reshape.540), calls=%async_computation.3 | async-start | bytes 3145728 | tf_op jit(solution)/shard_map/all_to_all | solution.py:284
  1006.0 242.2 %reduce-scatter.10.cloned.1.call-start = ((), (), s32[]{:S(2)}) async-start(), calls=%async_computation.11 | async-start | bytes 974848
  1007.4 271.5 %all-reduce.24.cloned.1.call-start = ((), (), s32[]{:S(2)}) async-start(), calls=%async_computation.12 | async-start | bytes 1916928 | tf_op jit(solution)/shard_map/psum | solution.py:288
  (30 other events, 193.4 us)
Sparse Core Ops, SparseCore 0:
  10.8 133.4 all-gather.3
  147.1 61.9 all-gather.5
  529.9 134.9 reduce-scatter.7
  897.8 232.4 reduce-scatter.5
  1133.0 76.9 reduce-scatter.9
  1212.4 15.9 all-reduce.23
